TPU v7x, 128 devices: a whole 4x4x4 slice. The times are simulated.
128 devices in a mesh: req: 4 (over x), exp: 32 (over z, y, core).
Axes of the slice: x: 4, y: 4, z: 4, core: 2. Of those that a mesh axis runs over, the one named last changes fastest.
Arguments:
- hidden_in: bfloat16 [4, 32, 128, 2048], P('req', 'exp'), may hold values from -6 to 6
- queries: bfloat16 [4, 32, 128, 2048], P('req', 'exp'), may hold values from -6 to 6
- suffix_pairs: bfloat16 [4, 32, 2, 128, 2048], P('req', 'exp'), may hold values from -6 to 6
- prefix_cache: bfloat16 [32, 4, 2, 384, 2048], P('exp', 'req'), may hold values from -6 to 6
- suffix_length: int32 [4, 32], P('req', 'exp'), may hold values from 1 to 128, 3072 in all within a row
- request_group: int32 [4, 32], P('req', 'exp'), may hold values from 0 to 3
- prefix_owner: int32 [32, 4], P('exp'), may hold values from 0 to 3, each once within a row
- out_weight: bfloat16 [2048, 2048], replicated, may hold values from -0.8984375 to 0.8984375
- norm_gain: float32 [2048], replicated, may hold values from 0.1 to 1.9
- routes: int32 [4, 32, 128, 8], P('req', 'exp'), may hold values from 0 to 31, all different within a row; in each aligned block of 128 rows (0 to 127, 128 to 255, ..., all dimensions but the last counted through in order) at most 40 rows name the same one
- gate_values: float32 [4, 32, 128, 8], P('req', 'exp'), may hold values from 0.05 to 0.3
- expert_upward: bfloat16 [32, 2048, 2048], P('exp'), may hold values from -0.125 to 0.125
- expert_downward: bfloat16 [32, 1024, 2048], P('exp'), may hold values from -0.1875 to 0.1875
Outputs:
- layer_out: bfloat16 [4, 32, 128, 2048], P('req', 'exp')
Inputs may be any that keep to these rules, and one draw needn't show every extreme that they name: The request at row r and column e reads the group held at prefix_cache[e, prefix_owner[e, request_group[r, e]]]. `prefix_owner`: each row is a permutation of 0 to 3. `routes`: a row names 8 different experts; on the rows of one device no expert is named more than 40 times, and on the rows of some device one expert is named exactly 40 times.
All inputs are finite; a program needn't handle non-finite values. No bound on the sum of `suffix_length` on one device may be relied on, other than what follows from the above.
Results may differ from a plain program's by a relative error of at most 0.0052.
Values may be sent and summed in bfloat16 or wider, within the bound.
A program may use at most 128 MiB of HBM per device.

v0:
```python
import jax
import jax.numpy as jnp
from jax import lax
from jax.sharding import PartitionSpec as P

HD = 128
SINK = 4


def softmax_part(scores, visible, values):
    masked = jnp.where(visible[None], scores, -jnp.inf)
    largest = jnp.max(masked, axis=2)
    weights = jnp.exp(masked - largest[:, :, None])
    totals = jnp.sum(weights, axis=2)
    summed = jnp.einsum(
        "htc,chd->htd", weights.astype(jnp.bfloat16), values, preferred_element_type=jnp.float32
    )
    return (largest, totals, summed)


def prefix_part(query_heads, cache):
    row_count = query_heads.shape[0]
    head_count = query_heads.shape[1]
    window = cache.shape[1]
    cache_keys = cache[0].reshape(window, head_count, HD)
    cache_values = cache[1].reshape(window, head_count, HD)
    scores = jnp.einsum(
        "thd,chd->htc", query_heads, cache_keys, preferred_element_type=jnp.float32
    ) * HD ** (-0.5)
    column = lax.broadcasted_iota(jnp.int32, (row_count, window), 1)
    position = lax.broadcasted_iota(jnp.int32, (row_count, window), 0)
    return softmax_part(scores, (column < SINK) | (column > position), cache_values)


def suffix_part(query_heads, pairs):
    row_count = query_heads.shape[0]
    head_count = query_heads.shape[1]
    own_keys = pairs[0].reshape(row_count, head_count, HD)
    own_values = pairs[1].reshape(row_count, head_count, HD)
    scores = jnp.einsum(
        "thd,shd->hts", query_heads, own_keys, preferred_element_type=jnp.float32
    ) * HD ** (-0.5)
    column = lax.broadcasted_iota(jnp.int32, (row_count, row_count), 1)
    position = lax.broadcasted_iota(jnp.int32, (row_count, row_count), 0)
    visible = column <= position
    return softmax_part(scores, visible, own_values)


def merge_parts(first, second):
    largest = jnp.maximum(first[0], second[0])
    scale_first = jnp.exp(first[0] - largest)
    scale_second = jnp.exp(second[0] - largest)
    totals = first[1] * scale_first + second[1] * scale_second
    summed = first[2] * scale_first[:, :, None] + second[2] * scale_second[:, :, None]
    merged = summed / totals[:, :, None]
    head_count = merged.shape[0]
    row_count = merged.shape[1]
    return jnp.transpose(merged, (1, 0, 2)).reshape(row_count, head_count * HD).astype(jnp.bfloat16)


def on_device(
    hidden_in,
    queries,
    suffix_pairs,
    prefix_cache,
    suffix_length,
    request_group,
    prefix_owner,
    out_weight,
    norm_gain,
    routes,
    gate_values,
    expert_upward,
    expert_downward,
):
    row_count = hidden_in.shape[2]
    width = hidden_in.shape[3]
    head_count = width // HD
    query_rows = queries[0, 0]
    query_heads = query_rows.reshape(row_count, head_count, HD)
    owner = prefix_owner[0, request_group[0, 0]]
    blank_stats = jnp.zeros((head_count, row_count), jnp.float32)
    blank_sums = jnp.zeros((head_count, row_count, HD), jnp.float32)
    carry = (blank_stats, blank_stats, blank_sums)
    piece = lax.all_gather(prefix_cache, "req", axis=1, tiled=True)
    start = jnp.int32(0)
    held = piece.shape[1]
    inside = (owner >= start) & (owner < start + held)
    offset = jnp.clip(owner, 0, held - 1)

    def attend_piece(ignored):
        cache = lax.dynamic_index_in_dim(piece[0], offset, 0, keepdims=False)
        return prefix_part(query_heads, cache)

    def keep_carry(ignored):
        return carry

    prefix_stats = lax.cond(inside, attend_piece, keep_carry, 0)
    suffix_stats = suffix_part(query_heads, suffix_pairs[0, 0])
    attention = merge_parts(prefix_stats, suffix_stats)
    mixed = jnp.dot(attention, out_weight, preferred_element_type=jnp.float32)
    residual = hidden_in[0, 0].astype(jnp.float32) + mixed
    scaled = residual * lax.rsqrt(jnp.mean(residual * residual, axis=1, keepdims=True) + 1e-05)
    normed = (scaled * norm_gain[None, :]).astype(jnp.bfloat16)
    flat_routes = routes[0, 0].reshape(-1)
    entry_count = flat_routes.shape[0]
    top_count = routes.shape[3]
    column_count = lax.axis_size("exp")
    local_count = expert_downward.shape[0]
    expert_count = local_count * column_count
    capacity = min(row_count, (row_count * top_count * 5 // (4 * expert_count) + 7) // 8 * 8)
    expert_ids = jnp.arange(expert_count, dtype=jnp.int32)
    chosen = (flat_routes[:, None] == expert_ids[None, :]).astype(jnp.int32)
    earlier = jnp.cumsum(chosen, axis=0) - chosen
    slot_rank = jnp.sum(earlier * chosen, axis=1)
    slot_of = flat_routes * capacity + slot_rank
    slot_count = expert_count * capacity
    source = (
        jnp.full((slot_count,), entry_count, jnp.int32)
        .at[slot_of]
        .set(jnp.arange(entry_count, dtype=jnp.int32))
    )
    filled = source < entry_count
    token_of = jnp.minimum(source, entry_count - 1) // top_count
    outgoing_rows = jnp.where(filled[:, None], normed[token_of], jnp.zeros((), jnp.bfloat16))
    outgoing_rows = outgoing_rows.reshape(column_count, local_count, capacity, width)
    joined = jnp.einsum(
        "sekd,edf->sekf",
        lax.all_to_all(outgoing_rows, "exp", split_axis=0, concat_axis=0, tiled=True),
        expert_upward,
        preferred_element_type=jnp.float32,
    )
    inner_width = joined.shape[3] // 2
    hidden_units = (jax.nn.silu(joined[..., :inner_width]) * joined[..., inner_width:]).astype(
        jnp.bfloat16
    )
    produced = jnp.einsum(
        "sekf,efd->sekd", hidden_units, expert_downward, preferred_element_type=jnp.float32
    ).astype(jnp.bfloat16)
    returned_rows = lax.all_to_all(produced, "exp", split_axis=0, concat_axis=0, tiled=True)
    per_entry = returned_rows.reshape(slot_count, width)[slot_of].reshape(
        row_count, top_count, width
    )
    weighted = jnp.sum(per_entry.astype(jnp.float32) * gate_values[0, 0][:, :, None], axis=1)
    combined = residual + weighted
    live_rows = jnp.arange(row_count, dtype=jnp.int32) < suffix_length[0, 0]
    layer_out = jnp.where(live_rows[:, None], combined, 0.0).astype(jnp.bfloat16)
    return layer_out.reshape(1, 1, row_count, width)


def solution(mesh):
    in_specs = (
        P("req", "exp", None, None),
        P("req", "exp", None, None),
        P("req", "exp", None, None, None),
        P("exp", "req", None, None, None),
        P("req", "exp"),
        P("req", "exp"),
        P("exp", None),
        P(),
        P(),
        P("req", "exp", None, None),
        P("req", "exp", None, None),
        P("exp", None, None),
        P("exp", None, None),
    )
    out_specs = P("req", "exp", None, None)
    return jax.shard_map(
        on_device, mesh=mesh, in_specs=in_specs, out_specs=out_specs, check_vma=False
    )
```

profile of v0, /device:TPU:0, one launch (start us, length us, event | category | flops | bytes accessed | tf_op | source)
XLA Modules:
  0.0 357.6 jit_solution(14926072692612265860)
XLA Ops:
  6.5 0.7 all-gather.2.cloned.1.call-update
  9.8 0.8 copy.51
  10.8 1.3 copy.41
  12.8 9.0 %reduce-window.6 = s32[32,8,128]{2,1,0:T(8,128)S(1)} reduce-window(s32[32,8,128]{2,1,0:T(8,128)S(1)} %fusion.40, s32[]{:T(128)} %constant.26.clone.1), window={size=1x1x128 pad=0_0x0_0x127_0}, to_apply=%region_6.7 | reduce-window | flops 4161536 | bytes 262148 | tf_op jit(solution)/shard_map/reduce-window
  22.5 4.3 %scatter_custom_fusion = s32[1280]{0:T(1024)S(1)} fusion(s32[1024]{0:T(1024)S(1)} %bitcast.118, s32[1024]{0:T(1024)S(1)} %iota.53, s32[]{:T(128)} %constant.59.clone.1), kind=kCustom, calls=%fused_computation.73 | custom fusion | bytes 5124 | tf_op jit(solution)/shard_map/scatter | solution.py:121
  27.6 102.5 %all-gather.2.cloned.1.call-done = bf16[1,4,2,384,2048]{4,3,2,0,1:T(8,128)(2,1)} async-done(((bf16[1,1,2,384,2048]{4,3,2,0,1:T(8,128)(2,1)}), bf16[1,4,2,384,2048]{4,3,2,0,1:T(8,128)(2,1)}) %all-gather.2.cloned.1.call-update) | async-done | bytes 12582928 | tf_op jit(solution)/shard_map/all_gather | solution.py:85
  130.0 24.1 %conditional.1 = (f32[16,128]{1,0:T(8,128)}, f32[16,128]{1,0:T(8,128)S(1)}, f32[16,128,128]{1,2,0:T(8,128)S(1)}) conditional(s32[]{:T(128)} %convert_element_type.60, () %tuple.13, (s32[]{:T(128)}, bf16[1,4,2,384,2048]{4,3,2,0,1:T(8,128)(2,1)}, bf16[128,16,128]{0,2,1:T(8,128)(2,1)S(1)}) %tuple.30), branch_computations={%region_0.1_spmd, %region_1.4_spmd} | conditional | flops 411398528 | bytes 45843268 | solution.py:98
  130.2 16.7 %copy.42 = bf16[1,4,2,384,2048]{3,4,2,1,0:T(8,128)(2,1)} copy(bf16[1,4,2,384,2048]{4,3,2,0,1:T(8,128)(2,1)} %get-tuple-element.28) | data formatting | bytes 25165824 | tf_op jit(solution)/shard_map
  147.5 2.2 constant_dynamic-slice_fusion.1
  149.7 1.4 fusion.2
  151.1 1.7 fusion.3
  152.8 1.4 fusion.1
  154.2 0.8 multiply_add_fusion
  155.3 4.8 %multiply_reduce_fusion = (f32[128]{0:T(128)S(1)}, f32[128,2048]{1,0:T(8,128)S(1)}) fusion(bf16[128,2048]{0,1:T(8,128)(2,1)S(1)} %bitcast.112, bf16[2048,2048]{1,0:T(8,128)(2,1)} %param.22, bf16[1,1,128,2048]{3,2,1,0:T(8,128)(2,1)S(1)} %copy-done.3), kind=kOutput, calls=%fused_computation.42 | convolution fusion | flops 1074790272 | bytes 10486272 | tf_op jit(solution)/shard_map/dot_general | solution.py:101
  160.3 6.1 %gather_fusion = bf16[1280,2048]{1,0:T(8,128)(2,1)} fusion(bf16[128,2048]{1,0:T(8,128)(2,1)S(1)} %multiply_convert_fusion, s32[2048]{0:T(1024)S(1)} %pad_clamp_fusion), kind=kCustom, calls=%fused_computation | custom fusion | bytes 10490880 | tf_op jit(solution)/shard_map/gather | solution.py:125
  166.4 2.9 broadcast_select_fusion
  169.3 69.2 %all_to_all.10 = bf16[32,1,40,2048]{3,2,1,0:T(8,128)(2,1)S(1)} all-to-all(bf16[32,1,40,2048]{3,2,1,0:T(8,128)(2,1)S(1)} %broadcast_select_fusion), channel_id=1, replica_groups=mesh['req'=4,'exp'=32] {'exp'}, dimensions={0} | all-to-all | bytes 10485760 | tf_op jit(solution)/shard_map/all_to_all | solution.py:129
  238.6 13.9 %fusion.17 = f32[32,1,40,2048]{3,2,0,1:T(8,128)S(1)} fusion(bf16[1,2048,2048]{2,1,0:T(8,128)(2,1)} %param.26, bf16[32,1,40,2048]{3,2,1,0:T(8,128)(2,1)S(1)} %all_to_all.10), kind=kOutput, calls=%fused_computation.29 | convolution fusion | flops 10737418240 | bytes 24117248 | tf_op jit(solution)/shard_map/sekd,edf->sekf/dot_general | solution.py:127
  252.5 7.8 %convert_bitcast_fusion = bf16[32,1,40,2048]{3,2,1,0:T(8,128)(2,1)} fusion(bf16[1,1024,2048]{2,1,0:T(8,128)(2,1)S(1)} %copy-done.7, f32[32,1,40,2048]{3,2,0,1:T(8,128)S(1)} %fusion.17), kind=kOutput, calls=%fused_computation.27 | convolution fusion | flops 5379194880 | bytes 19922944 | tf_op jit(solution)/shard_map/sekf,efd->sekd/dot_general | solution.py:137
  260.2 5.2 %all-to-all-start.1 = ((bf16[32,1,40,2048]{3,2,1,0:T(8,128)(2,1)}), bf16[32,1,40,2048]{3,2,1,0:T(8,128)(2,1)}, u32[]{:S(2)}, u32[]{:S(2)}) async-start(bf16[32,1,40,2048]{3,2,1,0:T(8,128)(2,1)} %convert_bitcast_fusion), calls=%async_computation.1 | async-start | bytes 10485760 | tf_op jit(solution)/shard_map/all_to_all | solution.py:140
  266.3 64.9 %all-to-all-done.1 = bf16[32,1,40,2048]{3,2,1,0:T(8,128)(2,1)} async-done(((bf16[32,1,40,2048]{3,2,1,0:T(8,128)(2,1)}), bf16[32,1,40,2048]{3,2,1,0:T(8,128)(2,1)}, u32[]{:S(2)}, u32[]{:S(2)}) %all-to-all-start.1) | async-done | bytes 5242912 | tf_op jit(solution)/shard_map/all_to_all | solution.py:140
  331.1 12.1 %gather_fusion.1 = bf16[1024,2048]{1,0:T(8,128)(2,1)} fusion(bf16[1280,2048]{1,0:T(8,128)(2,1)} %bitcast.34, s32[1024]{0:T(1024)S(1)} %broadcast_clamp_fusion), kind=kCustom, calls=%fused_computation.1 | custom fusion | bytes 8392704 | tf_op jit(solution)/shard_map/gather | solution.py:141
  343.2 6.5 %fusion.12 = f32[128,2048]{1,0:T(8,128)S(1)} fusion(bf16[1024,2048]{1,0:T(8,128)(2,1)} %gather_fusion.1, f32[128,8]{1,0:T(8,128)S(1)} %copy.57), kind=kLoop, calls=%fused_computation.21 | loop fusion | flops 6029312 | bytes 5246976 | tf_op jit(solution)/shard_map/reduce_sum | solution.py:144
  349.7 1.0 fusion.35
  (51 shorter events, 3.6 us)
Async XLA Ops:
  6.5 1.4 copy-start
  6.5 5.5 %copy-start.2 = (bf16[1,1,2,128,2048]{4,3,2,1,0:T(8,128)(2,1)S(1)}, bf16[1,1,2,128,2048]{4,3,2,1,0:T(8,128)(2,1)}, u32[]{:S(2)}) copy-start(bf16[1,1,2,128,2048]{4,3,2,1,0:T(8,128)(2,1)} %param.17) | copy-start | bytes 3145732
  6.5 123.5 %all-gather.2.cloned.1.call-start = ((), (), s32[]{:S(2)}) async-start(), calls=%async_computation.2 | async-start | bytes 15728640 | tf_op jit(solution)/shard_map/all_gather | solution.py:85
  6.5 15.6 %copy-start.4 = (s32[1,1,128,8]{2,3,1,0:T(8,128)S(1)}, s32[1,1,128,8]{2,3,1,0:T(8,128)}, u32[]{:S(2)}) copy-start(s32[1,1,128,8]{2,3,1,0:T(8,128)} %param.24) | copy-start | bytes 12292
  154.2 1.2 copy-start.3
  155.3 4.8 %copy-start.5 = (f32[2048]{0:T(1024)S(1)}, f32[2048]{0:T(1024)}, u32[]{:S(2)}) copy-start(f32[2048]{0:T(1024)} %param.23) | copy-start | bytes 24580
  238.5 13.9 %copy-start.7 = (bf16[1,1024,2048]{2,1,0:T(8,128)(2,1)S(1)}, bf16[1,1024,2048]{2,1,0:T(8,128)(2,1)}, u32[]{:S(2)}) copy-start(bf16[1,1024,2048]{2,1,0:T(8,128)(2,1)} %param.27) | copy-start | bytes 12582916
  260.2 5.2 %copy-start.6 = (f32[1,1,128,8]{2,3,1,0:T(8,128)S(1)}, f32[1,1,128,8]{2,3,1,0:T(8,128)}, u32[]{:S(2)}) copy-start(f32[1,1,128,8]{2,3,1,0:T(8,128)} %param.25) | copy-start | bytes 12292
  260.2 70.9 %all-to-all-start.1 = ((bf16[32,1,40,2048]{3,2,1,0:T(8,128)(2,1)}), bf16[32,1,40,2048]{3,2,1,0:T(8,128)(2,1)}, u32[]{:S(2)}, u32[]{:S(2)}) async-start(bf16[32,1,40,2048]{3,2,1,0:T(8,128)(2,1)} %convert_bitcast_fusion), calls=%async_computation.1 | async-start | bytes 10485760 | tf_op jit(solution)/shard_map/all_to_all | solution.py:140
  331.1 19.6 %copy-start.1 = (s32[1,4]{1,0:T(1,128)S(1)}, s32[1,4]{1,0:T(1,128)}, u32[]{:S(2)}) copy-start(s32[1,4]{1,0:T(1,128)} %param.21) | copy-start | bytes 52
Sparse Core Ops, SparseCore 0:
  9.0 121.0 all-gather.1
where the time goes:
time: 359 us; the launch traced here: 358 us
  waiting for transfers between devices  168 us (47%)
  blocking collectives  69.2 us (19%)
  local copies, waits for them, and re-layouts  45.7 us (13%)
  matrix products  30.3 us (8%)
  other arithmetic  22.3 us (6%)
  between operations  16.2 us (5%)
  starting transfers between devices  5.22 us (1%)
    all_gather x1, waiting for transfers between devices, on_device(): piece = lax.all_gather(prefix_cache, 'req', axis=1, tiled=True)  102 us
    all_to_all x1, blocking collectives, on_device(): lax.all_to_all(outgoing_rows, 'exp', split_axis=0, concat_axis=0, tiled=T...  69.2 us
    all_to_all x1, waiting for transfers between devices, on_device(): lax.all_to_all(produced, 'exp', split_axis=0, concat_axis=0, tiled=True)  64.9 us
    another operation x3, local copies, waits for them, and re-layouts  16.8 us
    dot_general x1, matrix products, on_device(): jnp.einsum('sekd,edf->sekf', lax.all_to_all(outgoing_rows, 'exp', split_a...  13.9 us
    gather x1, local copies, waits for them, and re-layouts, on_device(): returned_rows.reshape(slot_count, width)[slot_of]  12.1 us
    another operation x3, other arithmetic  9.14 us
    dot_general x1, matrix products, on_device(): jnp.einsum('sekf,efd->sekd', hidden_units, expert_downward, preferred_ele...  7.78 us
  transfers between devices with their start and end apart: 2, of which 2 were waited for; matrix products, arithmetic and copies ran while one was open for 5% of the time, Pallas kernels for 0%

commit v1 on v0

--- a/solution.py
+++ b/solution.py
@@ -82,7 +82,9 @@
     blank_stats = jnp.zeros((head_count, row_count), jnp.float32)
     blank_sums = jnp.zeros((head_count, row_count, HD), jnp.float32)
     carry = (blank_stats, blank_stats, blank_sums)
-    piece = lax.all_gather(prefix_cache, "req", axis=1, tiled=True)
+    piece = jnp.concatenate(
+        lax.all_to_all(jnp.stack([prefix_cache] * lax.axis_size("req")), "req", 0, 0), axis=1
+    )
     start = jnp.int32(0)
     held = piece.shape[1]
     inside = (owner >= start) & (owner < start + held)

time: 359 us -> 360 us (level)
  waiting for transfers between devices: 168 us -> 185 us
  between operations: 16.2 us -> 2.88 us
  local copies, waits for them, and re-layouts: 45.7 us -> 36.3 us
  starting transfers between devices: 5.22 us -> 11.7 us
    all_to_all x0 -> x1, waiting for transfers between devices: none -> 120 us  [on_device(): lax.all_to_all(jnp.stack([prefix_cache] * lax.axis_size('req')), 'req', 0...]
    all_gather x1 -> x0, waiting for transfers between devices: 102 us -> none  [on_device(): piece = lax.all_gather(prefix_cache, 'req', axis=1, tiled=True)]
    another operation x3 -> x4, local copies, waits for them, and re-layouts: 16.8 us -> 9.1 us  [the longest x1 5.58 us: on_device(): jnp.stack([prefix_cache] * lax.axis_size('req'))]
    all_to_all x0 -> x1, starting transfers between devices: none -> 6.46 us  [on_device(): lax.all_to_all(jnp.stack([prefix_cache] * lax.axis_size('req')), 'req', 0...]
where the time goes in v1:
time: 360 us
  waiting for transfers between devices  185 us (51%)
  blocking collectives  70.5 us (20%)
  local copies, waits for them, and re-layouts  36.3 us (10%)
  matrix products  30.3 us (8%)
  other arithmetic  22.3 us (6%)
  starting transfers between devices  11.7 us (3%)
    all_to_all x1, waiting for transfers between devices, on_device(): lax.all_to_all(jnp.stack([prefix_cache] * lax.axis_size('req')), 'req', 0...  120 us
    all_to_all x1, blocking collectives, on_device(): lax.all_to_all(outgoing_rows, 'exp', split_axis=0, concat_axis=0, tiled=T...  70.5 us
    all_to_all x1, waiting for transfers between devices, on_device(): lax.all_to_all(produced, 'exp', split_axis=0, concat_axis=0, tiled=True)  64.9 us
    dot_general x1, matrix products, on_device(): jnp.einsum('sekd,edf->sekf', lax.all_to_all(outgoing_rows, 'exp', split_a...  13.9 us
    gather x1, local copies, waits for them, and re-layouts, on_device(): returned_rows.reshape(slot_count, width)[slot_of]  12.1 us
    another operation x3, other arithmetic  9.14 us
    dot_general x1, matrix products, on_device(): jnp.einsum('sekf,efd->sekd', hidden_units, expert_downward, preferred_ele...  7.78 us
  transfers between devices with their start and end apart: 2, of which 2 were waited for; matrix products, arithmetic and copies ran while one was open for 5% of the time, Pallas kernels for 0%

profile of v1, /device:TPU:0, one launch (start us, length us, event | category | flops | bytes accessed | tf_op | source)
XLA Modules:
  0.0 359.8 jit_solution(12396797390207524914)
XLA Ops:
  0.0 3.4 copy.40
  3.4 5.6 %stack.2 = bf16[4,1,1,2,384,2048]{4,5,3,2,1,0:T(8,128)(2,1)} broadcast(bf16[2,384,2048]{1,2,0:T(8,128)(2,1)S(1)} %copy.40), dimensions={3,4,5} | broadcast | bytes 15728640 | tf_op jit(solution)/shard_map/stack | solution.py:86
  9.0 6.5 %all-to-all-start = ((bf16[4,1,1,2,384,2048]{4,5,3,2,1,0:T(8,128)(2,1)}), bf16[4,1,1,2,384,2048]{4,5,3,2,1,0:T(8,128)(2,1)}, u32[]{:S(2)}, u32[]{:S(2)}) async-start(bf16[4,1,1,2,384,2048]{4,5,3,2,1,0:T(8,128)(2,1)} %stack.2), calls=%async_computation | async-start | bytes 25165824 | tf_op jit(solution)/shard_map/all_to_all | solution.py:86
  16.2 0.6 constant_dynamic-slice_fusion.2
  19.3 9.0 %reduce-window.6 = s32[32,8,128]{2,1,0:T(8,128)S(1)} reduce-window(s32[32,8,128]{2,1,0:T(8,128)S(1)} %fusion.40, s32[]{:T(128)} %constant.26.clone.1), window={size=1x1x128 pad=0_0x0_0x127_0}, to_apply=%region_6.7 | reduce-window | flops 4161536 | bytes 262148 | tf_op jit(solution)/shard_map/reduce-window
  29.1 4.3 %scatter_custom_fusion = s32[1280]{0:T(1024)S(1)} fusion(s32[1024]{0:T(1024)S(1)} %bitcast.118, s32[1024]{0:T(1024)S(1)} %iota.53, s32[]{:T(128)} %constant.59.clone.1), kind=kCustom, calls=%fused_computation.73 | custom fusion | bytes 5124 | tf_op jit(solution)/shard_map/scatter | solution.py:123
  34.1 120.4 %all-to-all-done = bf16[4,1,1,2,384,2048]{4,5,3,2,1,0:T(8,128)(2,1)} async-done(((bf16[4,1,1,2,384,2048]{4,5,3,2,1,0:T(8,128)(2,1)}), bf16[4,1,1,2,384,2048]{4,5,3,2,1,0:T(8,128)(2,1)}, u32[]{:S(2)}, u32[]{:S(2)}) %all-to-all-start) | async-done | bytes 12582944 | tf_op jit(solution)/shard_map/all_to_all | solution.py:86
  154.5 7.5 %conditional.1 = (f32[16,128]{1,0:T(8,128)}, f32[16,128]{1,0:T(8,128)S(1)}, f32[16,128,128]{1,2,0:T(8,128)S(1)}) conditional(s32[]{:T(128)} %convert_element_type.60, () %tuple.13, (s32[]{:T(128)}, bf16[4,1,1,2,384,2048]{4,5,3,2,1,0:T(8,128)(2,1)}, bf16[128,16,128]{0,2,1:T(8,128)(2,1)S(1)}) %tuple.28), branch_computations={%region_0.1_spmd, %region_1.4_spmd} | conditional | flops 411398528 | bytes 20677444 | solution.py:100
  155.2 2.2 constant_dynamic-slice_fusion.1
  157.4 1.4 fusion.2
  158.9 1.7 fusion.3
  160.6 1.4 fusion.1
  161.9 0.8 multiply_add_fusion
  163.1 4.8 %multiply_reduce_fusion = (f32[128]{0:T(128)S(1)}, f32[128,2048]{1,0:T(8,128)S(1)}) fusion(bf16[128,2048]{0,1:T(8,128)(2,1)S(1)} %bitcast.112, bf16[2048,2048]{1,0:T(8,128)(2,1)} %param.22, bf16[1,1,128,2048]{3,2,1,0:T(8,128)(2,1)S(1)} %copy-done.3), kind=kOutput, calls=%fused_computation.42 | convolution fusion | flops 1074790272 | bytes 10486272 | tf_op jit(solution)/shard_map/dot_general | solution.py:103
  168.0 6.1 %gather_fusion = bf16[1280,2048]{1,0:T(8,128)(2,1)} fusion(bf16[128,2048]{1,0:T(8,128)(2,1)S(1)} %multiply_convert_fusion, s32[2048]{0:T(1024)S(1)} %pad_clamp_fusion), kind=kCustom, calls=%fused_computation | custom fusion | bytes 10490880 | tf_op jit(solution)/shard_map/gather | solution.py:127
  174.2 2.9 broadcast_select_fusion
  177.1 70.5 %all_to_all.15 = bf16[32,1,40,2048]{3,2,1,0:T(8,128)(2,1)S(1)} all-to-all(bf16[32,1,40,2048]{3,2,1,0:T(8,128)(2,1)S(1)} %broadcast_select_fusion), channel_id=1, replica_groups=mesh['req'=4,'exp'=32] {'exp'}, dimensions={0} | all-to-all | bytes 10485760 | tf_op jit(solution)/shard_map/all_to_all | solution.py:131
  247.6 13.9 %fusion.17 = f32[32,1,40,2048]{3,2,0,1:T(8,128)S(1)} fusion(bf16[1,2048,2048]{2,1,0:T(8,128)(2,1)} %param.26, bf16[32,1,40,2048]{3,2,1,0:T(8,128)(2,1)S(1)} %all_to_all.15), kind=kOutput, calls=%fused_computation.29 | convolution fusion | flops 10737418240 | bytes 24117248 | tf_op jit(solution)/shard_map/sekd,edf->sekf/dot_general | solution.py:129
  261.5 7.8 %convert_bitcast_fusion = bf16[32,1,40,2048]{3,2,1,0:T(8,128)(2,1)} fusion(bf16[1,1024,2048]{2,1,0:T(8,128)(2,1)S(1)} %copy-done.8, f32[32,1,40,2048]{3,2,0,1:T(8,128)S(1)} %fusion.17), kind=kOutput, calls=%fused_computation.27 | convolution fusion | flops 5379194880 | bytes 19922944 | tf_op jit(solution)/shard_map/sekf,efd->sekd/dot_general | solution.py:139
  269.3 5.2 %all-to-all-start.2 = ((bf16[32,1,40,2048]{3,2,1,0:T(8,128)(2,1)}), bf16[32,1,40,2048]{3,2,1,0:T(8,128)(2,1)}, u32[]{:S(2)}, u32[]{:S(2)}) async-start(bf16[32,1,40,2048]{3,2,1,0:T(8,128)(2,1)} %convert_bitcast_fusion), calls=%async_computation.2 | async-start | bytes 10485760 | tf_op jit(solution)/shard_map/all_to_all | solution.py:142
  275.3 64.9 %all-to-all-done.2 = bf16[32,1,40,2048]{3,2,1,0:T(8,128)(2,1)} async-done(((bf16[32,1,40,2048]{3,2,1,0:T(8,128)(2,1)}), bf16[32,1,40,2048]{3,2,1,0:T(8,128)(2,1)}, u32[]{:S(2)}, u32[]{:S(2)}) %all-to-all-start.2) | async-done | bytes 5242912 | tf_op jit(solution)/shard_map/all_to_all | solution.py:142
  340.1 12.1 %gather_fusion.1 = bf16[1024,2048]{1,0:T(8,128)(2,1)} fusion(bf16[1280,2048]{1,0:T(8,128)(2,1)} %bitcast.34, s32[1024]{0:T(1024)S(1)} %broadcast_clamp_fusion), kind=kCustom, calls=%fused_computation.1 | custom fusion | bytes 8392704 | tf_op jit(solution)/shard_map/gather | solution.py:143
  352.2 6.5 %fusion.12 = f32[128,2048]{1,0:T(8,128)S(1)} fusion(bf16[1024,2048]{1,0:T(8,128)(2,1)} %gather_fusion.1, f32[128,8]{1,0:T(8,128)S(1)} %copy.56), kind=kLoop, calls=%fused_computation.21 | loop fusion | flops 6029312 | bytes 5246976 | tf_op jit(solution)/shard_map/reduce_sum | solution.py:146
  358.7 1.0 fusion.35
  (53 shorter events, 3.4 us)
Async XLA Ops:
  0.0 16.2 %copy-start = (s32[1,4]{1,0:T(1,128)S(1)}, s32[1,4]{1,0:T(1,128)}, u32[]{:S(2)}) copy-start(s32[1,4]{1,0:T(1,128)} %param.21) | copy-start | bytes 52
  9.0 9.0 %copy-start.5 = (s32[1,1,128,8]{2,3,1,0:T(8,128)S(1)}, s32[1,1,128,8]{2,3,1,0:T(8,128)}, u32[]{:S(2)}) copy-start(s32[1,1,128,8]{2,3,1,0:T(8,128)} %param.24) | copy-start | bytes 12292
  9.0 9.3 %copy-start.4 = (bf16[1,1,128,2048]{3,2,1,0:T(8,128)(2,1)S(1)}, bf16[1,1,128,2048]{3,2,1,0:T(8,128)(2,1)}, u32[]{:S(2)}) copy-start(bf16[1,1,128,2048]{3,2,1,0:T(8,128)(2,1)} %param.16) | copy-start | bytes 1572868
  9.0 9.6 %copy-start.2 = (bf16[1,1,2,128,2048]{4,3,2,1,0:T(8,128)(2,1)S(1)}, bf16[1,1,2,128,2048]{4,3,2,1,0:T(8,128)(2,1)}, u32[]{:S(2)}) copy-start(bf16[1,1,2,128,2048]{4,3,2,1,0:T(8,128)(2,1)} %param.17) | copy-start | bytes 3145732
  9.0 145.4 %all-to-all-start = ((bf16[4,1,1,2,384,2048]{4,5,3,2,1,0:T(8,128)(2,1)}), bf16[4,1,1,2,384,2048]{4,5,3,2,1,0:T(8,128)(2,1)}, u32[]{:S(2)}, u32[]{:S(2)}) async-start(bf16[4,1,1,2,384,2048]{4,5,3,2,1,0:T(8,128)(2,1)} %stack.2), calls=%async_computation | async-start | bytes 25165824 | tf_op jit(solution)/shard_map/all_to_all | solution.py:86
  161.9 1.2 copy-start.3
  163.1 4.8 %copy-start.6 = (f32[2048]{0:T(1024)S(1)}, f32[2048]{0:T(1024)}, u32[]{:S(2)}) copy-start(f32[2048]{0:T(1024)} %param.23) | copy-start | bytes 24580
  247.5 13.9 %copy-start.8 = (bf16[1,1024,2048]{2,1,0:T(8,128)(2,1)S(1)}, bf16[1,1024,2048]{2,1,0:T(8,128)(2,1)}, u32[]{:S(2)}) copy-start(bf16[1,1024,2048]{2,1,0:T(8,128)(2,1)} %param.27) | copy-start | bytes 12582916
  269.2 5.2 %copy-start.7 = (f32[1,1,128,8]{2,3,1,0:T(8,128)S(1)}, f32[1,1,128,8]{2,3,1,0:T(8,128)}, u32[]{:S(2)}) copy-start(f32[1,1,128,8]{2,3,1,0:T(8,128)} %param.25) | copy-start | bytes 12292
  269.3 70.9 %all-to-all-start.2 = ((bf16[32,1,40,2048]{3,2,1,0:T(8,128)(2,1)}), bf16[32,1,40,2048]{3,2,1,0:T(8,128)(2,1)}, u32[]{:S(2)}, u32[]{:S(2)}) async-start(bf16[32,1,40,2048]{3,2,1,0:T(8,128)(2,1)} %convert_bitcast_fusion), calls=%async_computation.2 | async-start | bytes 10485760 | tf_op jit(solution)/shard_map/all_to_all | solution.py:142
  340.1 19.6 %copy-start.1 = (s32[1,4]{1,0:T(1,128)S(1)}, s32[1,4]{1,0:T(1,128)}, u32[]{:S(2)}) copy-start(s32[1,4]{1,0:T(1,128)} %param.21) | copy-start | bytes 52
